TPU v7x, 512 devices: a whole 4x4x16 slice. The times are simulated.
512 devices in a mesh: slab: 128 (over x, z, core), ctrl: 4 (over y).
Axes of the slice: x: 4, y: 4, z: 16, core: 2. Of those that a mesh axis runs over, the one named last changes fastest.
Arguments:
- face_pressure: float32 [2097152], P(('slab', 'ctrl')), may hold values from 0 to 18
- face_area: float32 [3, 2097152], P(None, ('slab', 'ctrl')), may hold values from -0.00390625 to 0.00390625
- face_center: float32 [3, 2097152], P(None, ('slab', 'ctrl')), may hold values from -6 to 6
- motion: float32 [6], replicated, may hold values from -1 to 1
- inverse_mass: float32 [6], replicated, may hold values from 0.5 to 2
- control_points: float32 [3, 8192], P(None, ('slab', 'ctrl')), may hold values from -4 to 4
- control_modes: float32 [18, 8192], P(None, ('slab', 'ctrl')), may hold values from -0.25 to 0.25
- node_points: float32 [3, 1024, 32, 128], P(None, 'slab', 'ctrl'), may hold values from -5 to 5
- tile_list: int32 [1024, 32, 16], P('slab', 'ctrl'), may hold values from 0 to 63, as said below
- tile_count: int32 [1024, 32], P('slab', 'ctrl'), may hold values from 0 to 16, as said below
Outputs:
- node_shift: float32 [3, 1024, 32, 128], P(None, 'slab', 'ctrl')
- cell_volume: float32 [1024, 32, 128], P('slab', 'ctrl')
- volume_change: float32 [1024, 32, 128], P('slab', 'ctrl')
- new_state: float32 [6], replicated
Inputs may be any that keep to these rules, and one draw needn't show every extreme that they name: `tile_list`: the entries of one line are distinct tile numbers; only the first tile_count entries of a line are live, the others are to be ignored. `tile_count`: every line in the planes x with 3072 <= 8 x < 5120 has 16 live entries; every other line has at most 4.
All inputs are finite; a program needn't handle non-finite values.
Results may differ from a plain program's by a relative error of at most 0.0003.
Values sent between devices are 32-bit elements; how exact they have to be, the bound alone decides.
A program may use at most 64 MiB of HBM per device.

v0:
```python
import jax
import jax.numpy as jnp
from jax import lax
from jax.sharding import PartitionSpec as P

TILE = 128
TIME_STEP = 0.5
RADIUS = 4.0
GRAVITY = (0.0, 0.0, -0.5, 0.0, 0.0, 0.0)


def shifted(value, axis, by):
    devices = lax.axis_size(axis)
    pairs = [(i, i + by) for i in range(devices) if 0 <= i + by < devices]
    return lax.ppermute(value, axis, pairs)


def surface_loads(pressure, area, center):
    pushed = pressure[None, :] * area
    forces = jnp.sum(pushed, axis=1)
    moment_x = jnp.sum(center[1] * pushed[2] - center[2] * pushed[1])
    moment_y = jnp.sum(center[2] * pushed[0] - center[0] * pushed[2])
    moment_z = jnp.sum(center[0] * pushed[1] - center[1] * pushed[0])
    return jnp.concatenate([forces, jnp.stack([moment_x, moment_y, moment_z])])


def advance(total_loads, motion, inverse_mass):
    acceleration = inverse_mass * total_loads + jnp.array(GRAVITY, dtype=jnp.float32)
    new_state = motion + TIME_STEP * acceleration
    rigid_step = TIME_STEP * motion + 0.5 * TIME_STEP * TIME_STEP * acceleration
    return (new_state, rigid_step)


def mode_mix(rigid_step, modes):
    shaped = modes.reshape(6, 3, modes.shape[1])
    return jnp.einsum("k,kcj->cj", rigid_step, shaped, precision=lax.Precision.HIGHEST)


def kernel_sum(points, tile_ids, counts, center_tiles, coeff_tiles):
    longest = jnp.max(counts)

    def accumulate(entry_id, running):
        picked = jnp.take(tile_ids, entry_id, axis=1)
        centers = jnp.take(center_tiles, picked, axis=1)
        coeffs = jnp.take(coeff_tiles, picked, axis=1)
        square = jnp.zeros((points.shape[1], points.shape[2], centers.shape[2]), jnp.float32)
        for axis_id in range(3):
            offset = points[axis_id][:, :, None] - centers[axis_id][:, None, :]
            square = square + offset * offset
        radial = jnp.sqrt(square) / RADIUS
        falloff = jnp.maximum(1.0 - radial, 0.0)
        fourth = falloff * falloff
        fourth = fourth * fourth
        kernel = fourth * (4.0 * radial + 1.0)
        alive_mask = (entry_id < counts)[:, None, None]
        kernel = jnp.where(alive_mask, kernel, 0.0)
        return running + jnp.einsum("lnj,clj->cln", kernel, coeffs, precision=lax.Precision.HIGHEST)

    start = jnp.zeros((3, points.shape[1], points.shape[2]), jnp.float32)
    return lax.fori_loop(0, longest, accumulate, start)


def cell_volumes(lattice):
    span_x = lattice.shape[-3] - 1
    span_y = lattice.shape[-2] - 1
    corners = {}
    for shift_x in range(2):
        for shift_y in range(2):
            for shift_z in range(2):
                sliced = lattice[..., shift_x : shift_x + span_x, shift_y : shift_y + span_y, :]
                if shift_z == 1:
                    sliced = jnp.concatenate(
                        [sliced[..., 1:], jnp.zeros_like(sliced[..., :1])], axis=-1
                    )
                corners[shift_x, shift_y, shift_z] = sliced
    edge_x = 0.0
    edge_y = 0.0
    edge_z = 0.0
    for first in range(2):
        for second in range(2):
            edge_x = edge_x + corners[1, first, second] - corners[0, first, second]
            edge_y = edge_y + corners[first, 1, second] - corners[first, 0, second]
            edge_z = edge_z + corners[first, second, 1] - corners[first, second, 0]
    edge_x = 0.25 * edge_x
    edge_y = 0.25 * edge_y
    edge_z = 0.25 * edge_z
    ex0, ex1, ex2 = (edge_x[..., 0, :, :, :], edge_x[..., 1, :, :, :], edge_x[..., 2, :, :, :])
    ey0, ey1, ey2 = (edge_y[..., 0, :, :, :], edge_y[..., 1, :, :, :], edge_y[..., 2, :, :, :])
    ez0, ez1, ez2 = (edge_z[..., 0, :, :, :], edge_z[..., 1, :, :, :], edge_z[..., 2, :, :, :])
    return (
        ex0 * (ey1 * ez2 - ey2 * ez1)
        + ex1 * (ey2 * ez0 - ey0 * ez2)
        + ex2 * (ey0 * ez1 - ey1 * ez0)
    )


def local(
    face_pressure,
    face_area,
    face_center,
    motion,
    inverse_mass,
    control_points,
    control_modes,
    node_points,
    tile_list,
    tile_count,
):
    local_loads = surface_loads(face_pressure, face_area, face_center)
    centers_all, modes_all = (
        lax.all_gather(control_points, ("slab", "ctrl"), axis=1, tiled=True),
        lax.all_gather(control_modes, ("slab", "ctrl"), axis=1, tiled=True),
    )
    total_loads = lax.psum(local_loads, ("slab", "ctrl"))
    new_state, rigid_step = advance(total_loads, motion, inverse_mass)
    coeffs_all = mode_mix(rigid_step, modes_all)
    center_tiles = centers_all.reshape(3, -1, TILE)
    coeff_tiles = coeffs_all.reshape(3, -1, TILE)
    plane_count = node_points.shape[1]
    row_count = node_points.shape[2]
    line_nodes = node_points.shape[3]
    slots = tile_list.shape[2]
    node_shift = kernel_sum(
        node_points.reshape(3, -1, line_nodes),
        tile_list.reshape(-1, slots),
        tile_count.reshape(-1),
        center_tiles,
        coeff_tiles,
    ).reshape(node_points.shape)
    displaced = node_points + node_shift
    stacked = jnp.stack([node_points, displaced])
    next_plane = shifted(stacked[:, :, :1], "slab", -1)
    widened = jnp.concatenate([stacked, next_plane], axis=2)
    next_row = shifted(widened[:, :, :, :1], "ctrl", -1)
    extended = jnp.concatenate([widened, next_row], axis=3)
    volumes = cell_volumes(extended)
    plane_total = plane_count * lax.axis_size("slab")
    row_total = row_count * lax.axis_size("ctrl")
    plane_ids = lax.axis_index("slab") * plane_count + jnp.arange(plane_count, dtype=jnp.int32)
    row_ids = lax.axis_index("ctrl") * row_count + jnp.arange(row_count, dtype=jnp.int32)
    depth_ids = jnp.arange(line_nodes, dtype=jnp.int32)
    inside = (plane_ids < plane_total - 1)[:, None, None]
    inside = inside & (row_ids < row_total - 1)[None, :, None]
    inside = inside & (depth_ids < line_nodes - 1)[None, None, :]
    volumes = jnp.where(inside[None], volumes, 0.0)
    return (node_shift, volumes[1], volumes[1] - volumes[0], new_state)


def solution(mesh):
    placed = (
        P(("slab", "ctrl")),
        P(None, ("slab", "ctrl")),
        P(None, ("slab", "ctrl")),
        P(),
        P(),
        P(None, ("slab", "ctrl")),
        P(None, ("slab", "ctrl")),
        P(None, "slab", "ctrl", None),
        P("slab", "ctrl", None),
        P("slab", "ctrl"),
    )
    return jax.shard_map(
        local,
        mesh=mesh,
        in_specs=placed,
        out_specs=(
            P(None, "slab", "ctrl", None),
            P("slab", "ctrl", None),
            P("slab", "ctrl", None),
            P(),
        ),
        check_vma=False,
    )
```

profile of v0, /device:TPU:4, one launch (start us, length us, event | category | flops | bytes accessed | tf_op | source)
XLA Modules:
  0.0 821.4 jit_solution(15603495582386284360)
XLA Ops:
  0.6 1.0 fusion.60
  1.6 1.7 subtract_reduce_fusion.2
  3.3 2.0 pad_maximum_fusion.4
  5.3 108.6 %psum.7 = f32[6]{0:T(128)S(1)} all-reduce(f32[6]{0:T(128)S(1)} %pad_maximum_fusion.4), channel_id=1, replica_groups=mesh['slab'=128,'ctrl'=4] {'slab','ctrl'}, use_global_device_ids=true, to_apply=%region_5.0 | all-reduce | flops 6 | bytes 48 | tf_op jit(solution)/shard_map/psum | solution.py:114
  113.9 250.8 %all_gather.6 = f32[18,8192]{0,1:T(8,128)} all-gather(f32[18,16]{0,1:T(8,128)} %param.21), channel_id=1, replica_groups=mesh['slab'=128,'ctrl'=4] {'slab','ctrl'}, dimensions={1}, use_global_device_ids=true | all-gather | bytes 590976 | tf_op jit(solution)/shard_map/all_gather | solution.py:112
  364.8 2.9 copy.23
  368.4 1.1 fusion.43
  369.6 229.6 %all-gather = f32[512,16,3]{1,2,0:T(4,128)S(1)} all-gather(f32[1,16,3]{1,2,0:T(4,128)S(1)} %bitcast.94), channel_id=1, replica_groups=mesh['slab'=128,'ctrl'=4] {'slab','ctrl'}, dimensions={0}, use_global_device_ids=true | all-gather | bytes 98496 | tf_op jit(solution)/shard_map/all_gather | solution.py:111
  600.5 207.5 %while.13 = (s32[]{:T(128)}, f32[3,64,128]{2,0,1:T(4,128)S(1)}, s32[]{:T(128)}, s32[64,16]{0,1:T(8,128)S(1)}, f32[3,64,128]{2,0,1:T(4,128)S(1)}, /*index=5*/s32[...) while((s32[]{:T(128)}, f32[3,64,128]{2,0,1:T(4,128)S(1)}, ...), condition=%wide.region_7.9_spmd, body=%wide.region_6.8_spmd.sunk | while | flops 54601224 | bytes 1480693 | solution.py:60
  602.7 10.6 %fusion.70 = f32[3,64,128]{2,0,1:T(4,128)S(1)} fusion(f32[3,64,128]{2,0,1:T(4,128)S(1)} %get-tuple-element.258, f32[64,128]{1,0:T(8,128)S(1)} %bitcast.91, f32[64,128]{1,0:T(8,128)S(1)} %get-tuple-element.239, f32[64,128]{1,0:T(8,128)S(1)} %bitcast.92, f32[64,128]{1,0:T(8,128)S(1)} %get-tuple-element.241, f32[64,128]{1,0:T(8,128)S(1)} %bitcast.90, ...), kind=kOutput, calls=%fused_computation.31.clone.1 | convolution fusion | flops 54575104 | bytes 491648 | tf_op jit(solution)/shard_map/while/body/lnj,clj->cln/dot_general | solution.py:57
  615.7 10.6 %fusion.70 = f32[3,64,128]{2,0,1:T(4,128)S(1)} fusion(f32[3,64,128]{2,0,1:T(4,128)S(1)} %get-tuple-element.258, f32[64,128]{1,0:T(8,128)S(1)} %bitcast.91, f32[64,128]{1,0:T(8,128)S(1)} %get-tuple-element.239, f32[64,128]{1,0:T(8,128)S(1)} %bitcast.92, f32[64,128]{1,0:T(8,128)S(1)} %get-tuple-element.241, f32[64,128]{1,0:T(8,128)S(1)} %bitcast.90, ...), kind=kOutput, calls=%fused_computation.31.clone.1 | convolution fusion | flops 54575104 | bytes 491648 | tf_op jit(solution)/shard_map/while/body/lnj,clj->cln/dot_general | solution.py:57
  628.6 10.6 %fusion.70 = f32[3,64,128]{2,0,1:T(4,128)S(1)} fusion(f32[3,64,128]{2,0,1:T(4,128)S(1)} %get-tuple-element.258, f32[64,128]{1,0:T(8,128)S(1)} %bitcast.91, f32[64,128]{1,0:T(8,128)S(1)} %get-tuple-element.239, f32[64,128]{1,0:T(8,128)S(1)} %bitcast.92, f32[64,128]{1,0:T(8,128)S(1)} %get-tuple-element.241, f32[64,128]{1,0:T(8,128)S(1)} %bitcast.90, ...), kind=kOutput, calls=%fused_computation.31.clone.1 | convolution fusion | flops 54575104 | bytes 491648 | tf_op jit(solution)/shard_map/while/body/lnj,clj->cln/dot_general | solution.py:57
  641.5 10.6 %fusion.70 = f32[3,64,128]{2,0,1:T(4,128)S(1)} fusion(f32[3,64,128]{2,0,1:T(4,128)S(1)} %get-tuple-element.258, f32[64,128]{1,0:T(8,128)S(1)} %bitcast.91, f32[64,128]{1,0:T(8,128)S(1)} %get-tuple-element.239, f32[64,128]{1,0:T(8,128)S(1)} %bitcast.92, f32[64,128]{1,0:T(8,128)S(1)} %get-tuple-element.241, f32[64,128]{1,0:T(8,128)S(1)} %bitcast.90, ...), kind=kOutput, calls=%fused_computation.31.clone.1 | convolution fusion | flops 54575104 | bytes 491648 | tf_op jit(solution)/shard_map/while/body/lnj,clj->cln/dot_general | solution.py:57
  654.5 10.6 %fusion.70 = f32[3,64,128]{2,0,1:T(4,128)S(1)} fusion(f32[3,64,128]{2,0,1:T(4,128)S(1)} %get-tuple-element.258, f32[64,128]{1,0:T(8,128)S(1)} %bitcast.91, f32[64,128]{1,0:T(8,128)S(1)} %get-tuple-element.239, f32[64,128]{1,0:T(8,128)S(1)} %bitcast.92, f32[64,128]{1,0:T(8,128)S(1)} %get-tuple-element.241, f32[64,128]{1,0:T(8,128)S(1)} %bitcast.90, ...), kind=kOutput, calls=%fused_computation.31.clone.1 | convolution fusion | flops 54575104 | bytes 491648 | tf_op jit(solution)/shard_map/while/body/lnj,clj->cln/dot_general | solution.py:57
  665.9 0.7 gather_fusion
  666.7 0.7 gather_fusion.1
  667.4 10.6 %fusion.70 = f32[3,64,128]{2,0,1:T(4,128)S(1)} fusion(f32[3,64,128]{2,0,1:T(4,128)S(1)} %get-tuple-element.258, f32[64,128]{1,0:T(8,128)S(1)} %bitcast.91, f32[64,128]{1,0:T(8,128)S(1)} %get-tuple-element.239, f32[64,128]{1,0:T(8,128)S(1)} %bitcast.92, f32[64,128]{1,0:T(8,128)S(1)} %get-tuple-element.241, f32[64,128]{1,0:T(8,128)S(1)} %bitcast.90, ...), kind=kOutput, calls=%fused_computation.31.clone.1 | convolution fusion | flops 54575104 | bytes 491648 | tf_op jit(solution)/shard_map/while/body/lnj,clj->cln/dot_general | solution.py:57
  680.3 10.6 %fusion.70 = f32[3,64,128]{2,0,1:T(4,128)S(1)} fusion(f32[3,64,128]{2,0,1:T(4,128)S(1)} %get-tuple-element.258, f32[64,128]{1,0:T(8,128)S(1)} %bitcast.91, f32[64,128]{1,0:T(8,128)S(1)} %get-tuple-element.239, f32[64,128]{1,0:T(8,128)S(1)} %bitcast.92, f32[64,128]{1,0:T(8,128)S(1)} %get-tuple-element.241, f32[64,128]{1,0:T(8,128)S(1)} %bitcast.90, ...), kind=kOutput, calls=%fused_computation.31.clone.1 | convolution fusion | flops 54575104 | bytes 491648 | tf_op jit(solution)/shard_map/while/body/lnj,clj->cln/dot_general | solution.py:57
  693.3 10.6 %fusion.70 = f32[3,64,128]{2,0,1:T(4,128)S(1)} fusion(f32[3,64,128]{2,0,1:T(4,128)S(1)} %get-tuple-element.258, f32[64,128]{1,0:T(8,128)S(1)} %bitcast.91, f32[64,128]{1,0:T(8,128)S(1)} %get-tuple-element.239, f32[64,128]{1,0:T(8,128)S(1)} %bitcast.92, f32[64,128]{1,0:T(8,128)S(1)} %get-tuple-element.241, f32[64,128]{1,0:T(8,128)S(1)} %bitcast.90, ...), kind=kOutput, calls=%fused_computation.31.clone.1 | convolution fusion | flops 54575104 | bytes 491648 | tf_op jit(solution)/shard_map/while/body/lnj,clj->cln/dot_general | solution.py:57
  706.2 10.6 %fusion.70 = f32[3,64,128]{2,0,1:T(4,128)S(1)} fusion(f32[3,64,128]{2,0,1:T(4,128)S(1)} %get-tuple-element.258, f32[64,128]{1,0:T(8,128)S(1)} %bitcast.91, f32[64,128]{1,0:T(8,128)S(1)} %get-tuple-element.239, f32[64,128]{1,0:T(8,128)S(1)} %bitcast.92, f32[64,128]{1,0:T(8,128)S(1)} %get-tuple-element.241, f32[64,128]{1,0:T(8,128)S(1)} %bitcast.90, ...), kind=kOutput, calls=%fused_computation.31.clone.1 | convolution fusion | flops 54575104 | bytes 491648 | tf_op jit(solution)/shard_map/while/body/lnj,clj->cln/dot_general | solution.py:57
  719.1 10.6 %fusion.70 = f32[3,64,128]{2,0,1:T(4,128)S(1)} fusion(f32[3,64,128]{2,0,1:T(4,128)S(1)} %get-tuple-element.258, f32[64,128]{1,0:T(8,128)S(1)} %bitcast.91, f32[64,128]{1,0:T(8,128)S(1)} %get-tuple-element.239, f32[64,128]{1,0:T(8,128)S(1)} %bitcast.92, f32[64,128]{1,0:T(8,128)S(1)} %get-tuple-element.241, f32[64,128]{1,0:T(8,128)S(1)} %bitcast.90, ...), kind=kOutput, calls=%fused_computation.31.clone.1 | convolution fusion | flops 54575104 | bytes 491648 | tf_op jit(solution)/shard_map/while/body/lnj,clj->cln/dot_general | solution.py:57
  732.1 10.6 %fusion.70 = f32[3,64,128]{2,0,1:T(4,128)S(1)} fusion(f32[3,64,128]{2,0,1:T(4,128)S(1)} %get-tuple-element.258, f32[64,128]{1,0:T(8,128)S(1)} %bitcast.91, f32[64,128]{1,0:T(8,128)S(1)} %get-tuple-element.239, f32[64,128]{1,0:T(8,128)S(1)} %bitcast.92, f32[64,128]{1,0:T(8,128)S(1)} %get-tuple-element.241, f32[64,128]{1,0:T(8,128)S(1)} %bitcast.90, ...), kind=kOutput, calls=%fused_computation.31.clone.1 | convolution fusion | flops 54575104 | bytes 491648 | tf_op jit(solution)/shard_map/while/body/lnj,clj->cln/dot_general | solution.py:57
  743.4 0.7 gather_fusion
  745.0 10.6 %fusion.70 = f32[3,64,128]{2,0,1:T(4,128)S(1)} fusion(f32[3,64,128]{2,0,1:T(4,128)S(1)} %get-tuple-element.258, f32[64,128]{1,0:T(8,128)S(1)} %bitcast.91, f32[64,128]{1,0:T(8,128)S(1)} %get-tuple-element.239, f32[64,128]{1,0:T(8,128)S(1)} %bitcast.92, f32[64,128]{1,0:T(8,128)S(1)} %get-tuple-element.241, f32[64,128]{1,0:T(8,128)S(1)} %bitcast.90, ...), kind=kOutput, calls=%fused_computation.31.clone.1 | convolution fusion | flops 54575104 | bytes 491648 | tf_op jit(solution)/shard_map/while/body/lnj,clj->cln/dot_general | solution.py:57
  757.9 10.6 %fusion.70 = f32[3,64,128]{2,0,1:T(4,128)S(1)} fusion(f32[3,64,128]{2,0,1:T(4,128)S(1)} %get-tuple-element.258, f32[64,128]{1,0:T(8,128)S(1)} %bitcast.91, f32[64,128]{1,0:T(8,128)S(1)} %get-tuple-element.239, f32[64,128]{1,0:T(8,128)S(1)} %bitcast.92, f32[64,128]{1,0:T(8,128)S(1)} %get-tuple-element.241, f32[64,128]{1,0:T(8,128)S(1)} %bitcast.90, ...), kind=kOutput, calls=%fused_computation.31.clone.1 | convolution fusion | flops 54575104 | bytes 491648 | tf_op jit(solution)/shard_map/while/body/lnj,clj->cln/dot_general | solution.py:57
  770.9 10.6 %fusion.70 = f32[3,64,128]{2,0,1:T(4,128)S(1)} fusion(f32[3,64,128]{2,0,1:T(4,128)S(1)} %get-tuple-element.258, f32[64,128]{1,0:T(8,128)S(1)} %bitcast.91, f32[64,128]{1,0:T(8,128)S(1)} %get-tuple-element.239, f32[64,128]{1,0:T(8,128)S(1)} %bitcast.92, f32[64,128]{1,0:T(8,128)S(1)} %get-tuple-element.241, f32[64,128]{1,0:T(8,128)S(1)} %bitcast.90, ...), kind=kOutput, calls=%fused_computation.31.clone.1 | convolution fusion | flops 54575104 | bytes 491648 | tf_op jit(solution)/shard_map/while/body/lnj,clj->cln/dot_general | solution.py:57
  783.8 10.6 %fusion.70 = f32[3,64,128]{2,0,1:T(4,128)S(1)} fusion(f32[3,64,128]{2,0,1:T(4,128)S(1)} %get-tuple-element.258, f32[64,128]{1,0:T(8,128)S(1)} %bitcast.91, f32[64,128]{1,0:T(8,128)S(1)} %get-tuple-element.239, f32[64,128]{1,0:T(8,128)S(1)} %bitcast.92, f32[64,128]{1,0:T(8,128)S(1)} %get-tuple-element.241, f32[64,128]{1,0:T(8,128)S(1)} %bitcast.90, ...), kind=kOutput, calls=%fused_computation.31.clone.1 | convolution fusion | flops 54575104 | bytes 491648 | tf_op jit(solution)/shard_map/while/body/lnj,clj->cln/dot_general | solution.py:57
  796.7 10.6 %fusion.70 = f32[3,64,128]{2,0,1:T(4,128)S(1)} fusion(f32[3,64,128]{2,0,1:T(4,128)S(1)} %get-tuple-element.258, f32[64,128]{1,0:T(8,128)S(1)} %bitcast.91, f32[64,128]{1,0:T(8,128)S(1)} %get-tuple-element.239, f32[64,128]{1,0:T(8,128)S(1)} %bitcast.92, f32[64,128]{1,0:T(8,128)S(1)} %get-tuple-element.241, f32[64,128]{1,0:T(8,128)S(1)} %bitcast.90, ...), kind=kOutput, calls=%fused_computation.31.clone.1 | convolution fusion | flops 54575104 | bytes 491648 | tf_op jit(solution)/shard_map/while/body/lnj,clj->cln/dot_general | solution.py:57
  808.7 4.3 collective-permute-start
  813.8 0.7 collective-permute-done
  814.5 1.3 collective-permute-start.1
  815.9 4.3 collective-permute-done.1
  (149 shorter events, 27.7 us)
Async XLA Ops:
  364.7 3.7 copy-start.3
  364.7 3.7 copy-start.4
  364.7 3.7 copy-start.5
  364.7 4.9 copy-start.6
  367.6 232.0 %copy-start.1 = (s32[8,8,16]{2,1,0:T(8,128)S(1)}, s32[8,8,16]{2,1,0:T(8,128)}, u32[]{:S(2)}) copy-start(s32[8,8,16]{2,1,0:T(8,128)} %param.23) | copy-start | bytes 12292
  367.6 232.1 %copy-start.2 = (s32[8,8]{1,0:T(8,128)S(1)}, s32[8,8]{1,0:T(8,128)}, u32[]{:S(2)}) copy-start(s32[8,8]{1,0:T(8,128)} %param.24) | copy-start | bytes 772
  367.7 232.8 %copy-start = (f32[3,8,8,128]{3,2,1,0:T(8,128)S(1)}, f32[3,8,8,128]{3,2,1,0:T(8,128)}, u32[]{:S(2)}) copy-start(f32[3,8,8,128]{3,2,1,0:T(8,128)} %param.22) | copy-start | bytes 294916
  808.7 5.8 collective-permute-start
  814.5 5.8 collective-permute-start.1
where the time goes:
time: 822 us; the launch traced here: 821 us
  blocking collectives  589 us (72%)
  matrix products  171 us (21%)
  local copies, waits for them, and re-layouts  26.9 us (3%)
  loops' own time  12.4 us (2%)
  other arithmetic  10.3 us (1%)
    all_gather x1, blocking collectives, local(): lax.all_gather(control_modes, ('slab', 'ctrl'), axis=1, tiled=True)  251 us
    all_gather x1, blocking collectives, local(): lax.all_gather(control_points, ('slab', 'ctrl'), axis=1, tiled=True)  230 us
    dot_general x16, matrix products, accumulate(): jnp.einsum('lnj,clj->cln', kernel, coeffs, precision=lax.Precision.HIGHEST)  170 us
    psum x1, blocking collectives, local(): total_loads = lax.psum(local_loads, ('slab', 'ctrl'))  109 us
  transfers between devices with their start and end apart: 2, of which 2 were waited for; matrix products, arithmetic and copies ran while one was open for 0% of the time, Pallas kernels for 0%

commit v1 on v0

--- a/solution.py
+++ b/solution.py
@@ -7,6 +7,11 @@
 TIME_STEP = 0.5
 RADIUS = 4.0
 GRAVITY = (0.0, 0.0, -0.5, 0.0, 0.0, 0.0)
+
+
+def gather_over(value, mesh_axis, dim):
+    outgoing = jnp.stack([value] * lax.axis_size(mesh_axis))
+    return jnp.concatenate(lax.all_to_all(outgoing, mesh_axis, 0, 0), axis=dim)
 
 
 def shifted(value, axis, by):
@@ -109,7 +114,7 @@
     local_loads = surface_loads(face_pressure, face_area, face_center)
     centers_all, modes_all = (
         lax.all_gather(control_points, ("slab", "ctrl"), axis=1, tiled=True),
-        lax.all_gather(control_modes, ("slab", "ctrl"), axis=1, tiled=True),
+        gather_over(control_modes, ("slab", "ctrl"), 1),
     )
     total_loads = lax.psum(local_loads, ("slab", "ctrl"))
     new_state, rigid_step = advance(total_loads, motion, inverse_mass)

time: 822 us -> 620 us (0.75)
  blocking collectives: 589 us -> 337 us
  local copies, waits for them, and re-layouts: 26.9 us -> 52.4 us
  starting transfers between devices: 5.56 us -> 28.9 us
    all_gather x1 -> x0, blocking collectives: 251 us -> none  [local(): lax.all_gather(control_modes, ('slab', 'ctrl'), axis=1, tiled=True)]
    all_to_all x0 -> x1, starting transfers between devices: none -> 23.3 us  [gather_over(): return jnp.concatenate(lax.all_to_all(outgoing, mesh_axis, 0, 0), axis=dim)]
    unnamed x15 -> x26, local copies, waits for them, and re-layouts: 0.48 us -> 12.9 us
    reshape x1 -> x2, local copies, waits for them, and re-layouts: 0.27 us -> 11.1 us  [gather_over(): return jnp.concatenate(lax.all_to_all(outgoing, mesh_axis, 0, 0), axis=dim)]
  transfers between devices with their start and end apart: 2 -> 3, of which waited for: 2 -> 2; matrix products, arithmetic and copies ran while one was open for 0% -> 1% of each run, Pallas kernels for 0% -> 0%
where the time goes in v1:
time: 620 us; the launch traced here: 619 us
  blocking collectives  337 us (54%)
  matrix products  171 us (28%)
  local copies, waits for them, and re-layouts  52.4 us (8%)
  starting transfers between devices  28.9 us (5%)
  loops' own time  12.4 us (2%)
  other arithmetic  11.1 us (2%)
    all_gather x1, blocking collectives, local(): lax.all_gather(control_points, ('slab', 'ctrl'), axis=1, tiled=True)  229 us
    dot_general x16, matrix products, accumulate(): jnp.einsum('lnj,clj->cln', kernel, coeffs, precision=lax.Precision.HIGHEST)  170 us
    psum x1, blocking collectives, local(): total_loads = lax.psum(local_loads, ('slab', 'ctrl'))  107 us
    all_to_all x1, starting transfers between devices, gather_over(): return jnp.concatenate(lax.all_to_all(outgoing, mesh_axis, 0, 0), axis=dim)  23.3 us
    unnamed x26, local copies, waits for them, and re-layouts  12.9 us
  transfers between devices with their start and end apart: 3, of which 2 were waited for; matrix products, arithmetic and copies ran while one was open for 1% of the time, Pallas kernels for 0%

profile of v1, /device:TPU:4, one launch (start us, length us, event | category | flops | bytes accessed | tf_op | source)
XLA Modules:
  0.0 619.5 jit_solution(17119985288479074876)
XLA Ops:
  1.3 2.2 broadcast_bitcast_fusion
  3.6 5.5 reshape.187
  9.1 23.3 %all-to-all-start = ((f32[512,1,288]{2,1,0:T(1,128)}), f32[512,1,288]{2,1,0:T(1,128)S(1)}, u32[]{:S(2)}, u32[]{:S(2)}) async-start(f32[512,1,288]{2,1,0:T(1,128)} %reshape.187), calls=%async_computation | async-start | bytes 1572864 | tf_op jit(solution)/shard_map/all_to_all | solution.py:14
  33.3 2.0 pad_maximum_fusion.4
  35.3 107.3 %psum.7 = f32[6]{0:T(128)S(1)} all-reduce(f32[6]{0:T(128)S(1)} %pad_maximum_fusion.4), channel_id=1, replica_groups=mesh['slab'=128,'ctrl'=4] {'slab','ctrl'}, use_global_device_ids=true, to_apply=%region_5.0 | all-reduce | flops 6 | bytes 48 | tf_op jit(solution)/shard_map/psum | solution.py:119
  142.6 229.4 %all-gather = f32[512,16,3]{1,2,0:T(4,128)S(1)} all-gather(f32[1,16,3]{1,2,0:T(4,128)S(1)} %bitcast.100), channel_id=1, replica_groups=mesh['slab'=128,'ctrl'=4] {'slab','ctrl'}, dimensions={0}, use_global_device_ids=true | all-gather | bytes 98496 | tf_op jit(solution)/shard_map/all_gather | solution.py:116
  374.5 2.6 reduce.4
  377.2 4.0 reshape.188
  381.1 4.5 bitcast_bitcast_fusion
  385.6 6.6 %copy.24 = f32[18,512,16]{2,1,0:T(8,128)} copy(f32[18,512,16]{0,2,1:T(8,128)} %bitcast_bitcast_fusion) | data formatting | bytes 1179648 | tf_op jit(solution)/shard_map/reshape | solution.py:14
  392.3 4.6 reshape_reshape.3
  398.5 207.5 %while.13 = (s32[]{:T(128)}, f32[3,64,128]{2,0,1:T(4,128)S(1)}, s32[]{:T(128)}, s32[64,16]{0,1:T(8,128)S(1)}, f32[3,64,128]{2,0,1:T(4,128)S(1)}, /*index=5*/s32[...) while((s32[]{:T(128)}, f32[3,64,128]{2,0,1:T(4,128)S(1)}, ...), condition=%wide.region_7.9_spmd, body=%wide.region_6.8_spmd.sunk | while | flops 54601224 | bytes 1480693 | solution.py:65
  400.8 10.6 %fusion.70 = f32[3,64,128]{2,0,1:T(4,128)S(1)} fusion(f32[3,64,128]{2,0,1:T(4,128)S(1)} %get-tuple-element.258, f32[64,128]{1,0:T(8,128)S(1)} %bitcast.97, f32[64,128]{1,0:T(8,128)S(1)} %get-tuple-element.239, f32[64,128]{1,0:T(8,128)S(1)} %bitcast.98, f32[64,128]{1,0:T(8,128)S(1)} %get-tuple-element.241, f32[64,128]{1,0:T(8,128)S(1)} %bitcast.96, ...), kind=kOutput, calls=%fused_computation.31.clone.1 | convolution fusion | flops 54575104 | bytes 491648 | tf_op jit(solution)/shard_map/while/body/lnj,clj->cln/dot_general | solution.py:62
  413.7 10.6 %fusion.70 = f32[3,64,128]{2,0,1:T(4,128)S(1)} fusion(f32[3,64,128]{2,0,1:T(4,128)S(1)} %get-tuple-element.258, f32[64,128]{1,0:T(8,128)S(1)} %bitcast.97, f32[64,128]{1,0:T(8,128)S(1)} %get-tuple-element.239, f32[64,128]{1,0:T(8,128)S(1)} %bitcast.98, f32[64,128]{1,0:T(8,128)S(1)} %get-tuple-element.241, f32[64,128]{1,0:T(8,128)S(1)} %bitcast.96, ...), kind=kOutput, calls=%fused_computation.31.clone.1 | convolution fusion | flops 54575104 | bytes 491648 | tf_op jit(solution)/shard_map/while/body/lnj,clj->cln/dot_general | solution.py:62
  426.7 10.6 %fusion.70 = f32[3,64,128]{2,0,1:T(4,128)S(1)} fusion(f32[3,64,128]{2,0,1:T(4,128)S(1)} %get-tuple-element.258, f32[64,128]{1,0:T(8,128)S(1)} %bitcast.97, f32[64,128]{1,0:T(8,128)S(1)} %get-tuple-element.239, f32[64,128]{1,0:T(8,128)S(1)} %bitcast.98, f32[64,128]{1,0:T(8,128)S(1)} %get-tuple-element.241, f32[64,128]{1,0:T(8,128)S(1)} %bitcast.96, ...), kind=kOutput, calls=%fused_computation.31.clone.1 | convolution fusion | flops 54575104 | bytes 491648 | tf_op jit(solution)/shard_map/while/body/lnj,clj->cln/dot_general | solution.py:62
  439.6 10.6 %fusion.70 = f32[3,64,128]{2,0,1:T(4,128)S(1)} fusion(f32[3,64,128]{2,0,1:T(4,128)S(1)} %get-tuple-element.258, f32[64,128]{1,0:T(8,128)S(1)} %bitcast.97, f32[64,128]{1,0:T(8,128)S(1)} %get-tuple-element.239, f32[64,128]{1,0:T(8,128)S(1)} %bitcast.98, f32[64,128]{1,0:T(8,128)S(1)} %get-tuple-element.241, f32[64,128]{1,0:T(8,128)S(1)} %bitcast.96, ...), kind=kOutput, calls=%fused_computation.31.clone.1 | convolution fusion | flops 54575104 | bytes 491648 | tf_op jit(solution)/shard_map/while/body/lnj,clj->cln/dot_general | solution.py:62
  452.5 10.6 %fusion.70 = f32[3,64,128]{2,0,1:T(4,128)S(1)} fusion(f32[3,64,128]{2,0,1:T(4,128)S(1)} %get-tuple-element.258, f32[64,128]{1,0:T(8,128)S(1)} %bitcast.97, f32[64,128]{1,0:T(8,128)S(1)} %get-tuple-element.239, f32[64,128]{1,0:T(8,128)S(1)} %bitcast.98, f32[64,128]{1,0:T(8,128)S(1)} %get-tuple-element.241, f32[64,128]{1,0:T(8,128)S(1)} %bitcast.96, ...), kind=kOutput, calls=%fused_computation.31.clone.1 | convolution fusion | flops 54575104 | bytes 491648 | tf_op jit(solution)/shard_map/while/body/lnj,clj->cln/dot_general | solution.py:62
  465.5 10.6 %fusion.70 = f32[3,64,128]{2,0,1:T(4,128)S(1)} fusion(f32[3,64,128]{2,0,1:T(4,128)S(1)} %get-tuple-element.258, f32[64,128]{1,0:T(8,128)S(1)} %bitcast.97, f32[64,128]{1,0:T(8,128)S(1)} %get-tuple-element.239, f32[64,128]{1,0:T(8,128)S(1)} %bitcast.98, f32[64,128]{1,0:T(8,128)S(1)} %get-tuple-element.241, f32[64,128]{1,0:T(8,128)S(1)} %bitcast.96, ...), kind=kOutput, calls=%fused_computation.31.clone.1 | convolution fusion | flops 54575104 | bytes 491648 | tf_op jit(solution)/shard_map/while/body/lnj,clj->cln/dot_general | solution.py:62
  478.4 10.6 %fusion.70 = f32[3,64,128]{2,0,1:T(4,128)S(1)} fusion(f32[3,64,128]{2,0,1:T(4,128)S(1)} %get-tuple-element.258, f32[64,128]{1,0:T(8,128)S(1)} %bitcast.97, f32[64,128]{1,0:T(8,128)S(1)} %get-tuple-element.239, f32[64,128]{1,0:T(8,128)S(1)} %bitcast.98, f32[64,128]{1,0:T(8,128)S(1)} %get-tuple-element.241, f32[64,128]{1,0:T(8,128)S(1)} %bitcast.96, ...), kind=kOutput, calls=%fused_computation.31.clone.1 | convolution fusion | flops 54575104 | bytes 491648 | tf_op jit(solution)/shard_map/while/body/lnj,clj->cln/dot_general | solution.py:62
  491.3 10.6 %fusion.70 = f32[3,64,128]{2,0,1:T(4,128)S(1)} fusion(f32[3,64,128]{2,0,1:T(4,128)S(1)} %get-tuple-element.258, f32[64,128]{1,0:T(8,128)S(1)} %bitcast.97, f32[64,128]{1,0:T(8,128)S(1)} %get-tuple-element.239, f32[64,128]{1,0:T(8,128)S(1)} %bitcast.98, f32[64,128]{1,0:T(8,128)S(1)} %get-tuple-element.241, f32[64,128]{1,0:T(8,128)S(1)} %bitcast.96, ...), kind=kOutput, calls=%fused_computation.31.clone.1 | convolution fusion | flops 54575104 | bytes 491648 | tf_op jit(solution)/shard_map/while/body/lnj,clj->cln/dot_general | solution.py:62
  504.3 10.6 %fusion.70 = f32[3,64,128]{2,0,1:T(4,128)S(1)} fusion(f32[3,64,128]{2,0,1:T(4,128)S(1)} %get-tuple-element.258, f32[64,128]{1,0:T(8,128)S(1)} %bitcast.97, f32[64,128]{1,0:T(8,128)S(1)} %get-tuple-element.239, f32[64,128]{1,0:T(8,128)S(1)} %bitcast.98, f32[64,128]{1,0:T(8,128)S(1)} %get-tuple-element.241, f32[64,128]{1,0:T(8,128)S(1)} %bitcast.96, ...), kind=kOutput, calls=%fused_computation.31.clone.1 | convolution fusion | flops 54575104 | bytes 491648 | tf_op jit(solution)/shard_map/while/body/lnj,clj->cln/dot_general | solution.py:62
  517.2 10.6 %fusion.70 = f32[3,64,128]{2,0,1:T(4,128)S(1)} fusion(f32[3,64,128]{2,0,1:T(4,128)S(1)} %get-tuple-element.258, f32[64,128]{1,0:T(8,128)S(1)} %bitcast.97, f32[64,128]{1,0:T(8,128)S(1)} %get-tuple-element.239, f32[64,128]{1,0:T(8,128)S(1)} %bitcast.98, f32[64,128]{1,0:T(8,128)S(1)} %get-tuple-element.241, f32[64,128]{1,0:T(8,128)S(1)} %bitcast.96, ...), kind=kOutput, calls=%fused_computation.31.clone.1 | convolution fusion | flops 54575104 | bytes 491648 | tf_op jit(solution)/shard_map/while/body/lnj,clj->cln/dot_general | solution.py:62
  530.1 10.6 %fusion.70 = f32[3,64,128]{2,0,1:T(4,128)S(1)} fusion(f32[3,64,128]{2,0,1:T(4,128)S(1)} %get-tuple-element.258, f32[64,128]{1,0:T(8,128)S(1)} %bitcast.97, f32[64,128]{1,0:T(8,128)S(1)} %get-tuple-element.239, f32[64,128]{1,0:T(8,128)S(1)} %bitcast.98, f32[64,128]{1,0:T(8,128)S(1)} %get-tuple-element.241, f32[64,128]{1,0:T(8,128)S(1)} %bitcast.96, ...), kind=kOutput, calls=%fused_computation.31.clone.1 | convolution fusion | flops 54575104 | bytes 491648 | tf_op jit(solution)/shard_map/while/body/lnj,clj->cln/dot_general | solution.py:62
  543.1 10.6 %fusion.70 = f32[3,64,128]{2,0,1:T(4,128)S(1)} fusion(f32[3,64,128]{2,0,1:T(4,128)S(1)} %get-tuple-element.258, f32[64,128]{1,0:T(8,128)S(1)} %bitcast.97, f32[64,128]{1,0:T(8,128)S(1)} %get-tuple-element.239, f32[64,128]{1,0:T(8,128)S(1)} %bitcast.98, f32[64,128]{1,0:T(8,128)S(1)} %get-tuple-element.241, f32[64,128]{1,0:T(8,128)S(1)} %bitcast.96, ...), kind=kOutput, calls=%fused_computation.31.clone.1 | convolution fusion | flops 54575104 | bytes 491648 | tf_op jit(solution)/shard_map/while/body/lnj,clj->cln/dot_general | solution.py:62
  556.0 10.6 %fusion.70 = f32[3,64,128]{2,0,1:T(4,128)S(1)} fusion(f32[3,64,128]{2,0,1:T(4,128)S(1)} %get-tuple-element.258, f32[64,128]{1,0:T(8,128)S(1)} %bitcast.97, f32[64,128]{1,0:T(8,128)S(1)} %get-tuple-element.239, f32[64,128]{1,0:T(8,128)S(1)} %bitcast.98, f32[64,128]{1,0:T(8,128)S(1)} %get-tuple-element.241, f32[64,128]{1,0:T(8,128)S(1)} %bitcast.96, ...), kind=kOutput, calls=%fused_computation.31.clone.1 | convolution fusion | flops 54575104 | bytes 491648 | tf_op jit(solution)/shard_map/while/body/lnj,clj->cln/dot_general | solution.py:62
  568.9 10.6 %fusion.70 = f32[3,64,128]{2,0,1:T(4,128)S(1)} fusion(f32[3,64,128]{2,0,1:T(4,128)S(1)} %get-tuple-element.258, f32[64,128]{1,0:T(8,128)S(1)} %bitcast.97, f32[64,128]{1,0:T(8,128)S(1)} %get-tuple-element.239, f32[64,128]{1,0:T(8,128)S(1)} %bitcast.98, f32[64,128]{1,0:T(8,128)S(1)} %get-tuple-element.241, f32[64,128]{1,0:T(8,128)S(1)} %bitcast.96, ...), kind=kOutput, calls=%fused_computation.31.clone.1 | convolution fusion | flops 54575104 | bytes 491648 | tf_op jit(solution)/shard_map/while/body/lnj,clj->cln/dot_general | solution.py:62
  581.9 10.6 %fusion.70 = f32[3,64,128]{2,0,1:T(4,128)S(1)} fusion(f32[3,64,128]{2,0,1:T(4,128)S(1)} %get-tuple-element.258, f32[64,128]{1,0:T(8,128)S(1)} %bitcast.97, f32[64,128]{1,0:T(8,128)S(1)} %get-tuple-element.239, f32[64,128]{1,0:T(8,128)S(1)} %bitcast.98, f32[64,128]{1,0:T(8,128)S(1)} %get-tuple-element.241, f32[64,128]{1,0:T(8,128)S(1)} %bitcast.96, ...), kind=kOutput, calls=%fused_computation.31.clone.1 | convolution fusion | flops 54575104 | bytes 491648 | tf_op jit(solution)/shard_map/while/body/lnj,clj->cln/dot_general | solution.py:62
  594.8 10.6 %fusion.70 = f32[3,64,128]{2,0,1:T(4,128)S(1)} fusion(f32[3,64,128]{2,0,1:T(4,128)S(1)} %get-tuple-element.258, f32[64,128]{1,0:T(8,128)S(1)} %bitcast.97, f32[64,128]{1,0:T(8,128)S(1)} %get-tuple-element.239, f32[64,128]{1,0:T(8,128)S(1)} %bitcast.98, f32[64,128]{1,0:T(8,128)S(1)} %get-tuple-element.241, f32[64,128]{1,0:T(8,128)S(1)} %bitcast.96, ...), kind=kOutput, calls=%fused_computation.31.clone.1 | convolution fusion | flops 54575104 | bytes 491648 | tf_op jit(solution)/shard_map/while/body/lnj,clj->cln/dot_general | solution.py:62
  606.8 4.3 collective-permute-start
  611.1 1.4 collective-permute-done
  612.5 1.3 collective-permute-start.1
  614.0 4.3 collective-permute-done.1
  (164 shorter events, 32.6 us)
Async XLA Ops:
  0.6 0.7 copy-start
  3.5 28.9 %copy-start.2 = (f32[3,4096]{1,0:T(4,128)S(1)}, f32[3,4096]{1,0:T(4,128)}, u32[]{:S(2)}) copy-start(f32[3,4096]{1,0:T(4,128)} %param.16) | copy-start | bytes 147460
  3.5 28.9 %copy-start.5 = (f32[4096]{0:T(1024)S(1)}, f32[4096]{0:T(1024)}, u32[]{:S(2)}) copy-start(f32[4096]{0:T(1024)} %param.15) | copy-start | bytes 49156
  3.5 29.0 %copy-start.3 = (f32[3,4096]{1,0:T(4,128)S(1)}, f32[3,4096]{1,0:T(4,128)}, u32[]{:S(2)}) copy-start(f32[3,4096]{1,0:T(4,128)} %param.17) | copy-start | bytes 147460
  3.5 139.1 %copy-start.10 = (f32[3,16]{1,0:T(4,128)S(1)}, f32[3,16]{1,0:T(4,128)}, u32[]{:S(2)}) copy-start(f32[3,16]{1,0:T(4,128)} %param.20) | copy-start | bytes 580
  3.5 369.0 %copy-start.4 = (s32[8,8,16]{2,1,0:T(8,128)S(1)}, s32[8,8,16]{2,1,0:T(8,128)}, u32[]{:S(2)}) copy-start(s32[8,8,16]{2,1,0:T(8,128)} %param.23) | copy-start | bytes 12292
  3.6 369.0 %copy-start.6 = (s32[8,8]{1,0:T(8,128)S(1)}, s32[8,8]{1,0:T(8,128)}, u32[]{:S(2)}) copy-start(s32[8,8]{1,0:T(8,128)} %param.24) | copy-start | bytes 772
  3.6 369.8 %copy-start.7 = (f32[6]{0:T(128)S(1)}, f32[6]{0:T(128)}, u32[]{:S(2)}) copy-start(f32[6]{0:T(128)} %param.18) | copy-start | bytes 76
  3.6 369.8 %copy-start.8 = (f32[6]{0:T(128)S(1)}, f32[6]{0:T(128)}, u32[]{:S(2)}) copy-start(f32[6]{0:T(128)} %param.19) | copy-start | bytes 76
  3.6 369.8 %copy-start.9 = (f32[6]{0:T(128)S(1)}, f32[6]{0:T(128)}, u32[]{:S(2)}) copy-start(f32[6]{0:T(128)} %constant.102.clone) | copy-start | bytes 76
  9.1 364.9 %all-to-all-start = ((f32[512,1,288]{2,1,0:T(1,128)}), f32[512,1,288]{2,1,0:T(1,128)S(1)}, u32[]{:S(2)}, u32[]{:S(2)}) async-start(f32[512,1,288]{2,1,0:T(1,128)} %reshape.187), calls=%async_computation | async-start | bytes 1572864 | tf_op jit(solution)/shard_map/all_to_all | solution.py:14
  392.3 6.3 %copy-start.1 = (f32[3,8,8,128]{3,2,1,0:T(8,128)S(1)}, f32[3,8,8,128]{3,2,1,0:T(8,128)}, u32[]{:S(2)}) copy-start(f32[3,8,8,128]{3,2,1,0:T(8,128)} %param.22) | copy-start | bytes 294916
  606.8 5.8 collective-permute-start
  612.5 5.8 collective-permute-start.1
